TPU v7x, 256 devices: a whole 4x4x8 slice. The times are simulated.
256 devices in a mesh: group: 16 (over x_hi, z), dev: 16 (over x_lo, y, core).
Axes of the slice: x: 4 (x_hi: 2, x_lo: 2; x = x_hi * 2 + x_lo), y: 4, z: 8, core: 2. Of those that a mesh axis runs over, the one named last changes fastest.
Arguments:
- expert_input: bfloat16 [2, 1536, 4096], P(None, ('group', 'dev')), may hold values from -6 to 6
- expert_ids: int32 [2, 1536, 2], P(None, ('group', 'dev')), may hold values from 0 to 7, all different within a row; in each aligned block of 6 rows (0 to 5, 6 to 11, ..., all dimensions but the last counted through in order) at most 2 rows name the same one
- combine: float32 [2, 1536, 2], P(None, ('group', 'dev')), may hold values from 0.25 to 1
- gate_weight: bfloat16 [16, 4096, 6144], P('dev', None, 'group'), may hold values from -0.09375 to 0.09375
- up_weight: bfloat16 [16, 4096, 6144], P('dev', None, 'group'), may hold values from -0.09375 to 0.09375
- down_weight: bfloat16 [16, 6144, 4096], P('dev', 'group'), may hold values from -0.0546875 to 0.0546875
Outputs:
- moe_out: bfloat16 [2, 1536, 4096], P(None, ('group', 'dev'))
Inputs may be any that keep to these rules, and one draw needn't show every extreme that they name: `expert_ids`: the two experts of a row differ; among the rows of one device in one step no expert is named more than 2 times.
All inputs are finite; a program needn't handle non-finite values.
Results may differ from a plain program's by a relative error of at most 0.017.
Values may be sent and summed in bfloat16 or wider, within the bound.
A program may use at most 64 MiB of HBM per device.

v0:
```python
import jax
import jax.numpy as jnp
from jax import lax
from jax.sharding import PartitionSpec as P


def local(expert_input, expert_ids, combine, gate_weight, up_weight, down_weight):
    dev_count = lax.axis_size("dev")
    row_count = expert_input.shape[1]
    step_count = expert_input.shape[0]
    experts = dev_count // 2
    slot_count = max(2, (2 * row_count + experts - 1) // experts)
    expert_iota = jnp.arange(experts, dtype=jnp.int32)
    owner_iota = jnp.arange(dev_count, dtype=jnp.int32) // 2
    slot_iota = jnp.arange(slot_count, dtype=jnp.int32)
    results = []
    for moment in range(step_count):
        chosen_ids = expert_ids[moment].reshape(-1)
        named_hits = (chosen_ids[:, None] == expert_iota[None, :]).astype(jnp.int32)
        earlier = jnp.cumsum(named_hits, 0) - named_hits
        position = jnp.sum(earlier * named_hits, 1)
        routed = (chosen_ids[None, None, :] == owner_iota[:, None, None]) & (
            position[None, None, :] == slot_iota[None, :, None]
        )
        routed_rows = routed.astype(jnp.float32).reshape(dev_count, slot_count, row_count, 2)
        row_pick = jnp.sum(routed_rows, 3).astype(jnp.bfloat16)
        outgoing = jnp.einsum(
            "dpj,jx->dpx", row_pick, expert_input[moment], preferred_element_type=jnp.float32
        ).astype(jnp.bfloat16)
        incoming = lax.all_to_all(outgoing, "dev", split_axis=0, concat_axis=0, tiled=True)
        shard_piece = lax.all_gather(incoming[None], "group", axis=0, tiled=True)
        flat_rows = shard_piece.reshape(-1, shard_piece.shape[-1])
        gate_val = jnp.dot(flat_rows, gate_weight[0], preferred_element_type=jnp.float32)
        up_val = jnp.dot(flat_rows, up_weight[0], preferred_element_type=jnp.float32)
        hidden = (jax.nn.silu(gate_val) * up_val).astype(jnp.bfloat16)
        product = jnp.dot(hidden, down_weight[0], preferred_element_type=jnp.float32)
        partial_value = product.reshape(shard_piece.shape)
        own_rows = lax.psum_scatter(
            partial_value.astype(jnp.bfloat16), "group", scatter_dimension=0, tiled=True
        ).astype(jnp.float32)
        halves = own_rows[0].astype(jnp.bfloat16)
        returned = lax.all_to_all(halves, "dev", split_axis=0, concat_axis=0, tiled=True)
        weights = jnp.einsum(
            "dpjk,jk->dpj", routed_rows, combine[moment], precision=lax.Precision.HIGHEST
        )
        blended = jnp.einsum(
            "dpj,dpx->jx", weights, returned.astype(jnp.float32), precision=lax.Precision.HIGHEST
        )
        results.append(blended.astype(jnp.bfloat16))
    return jnp.stack(results, 0)


def solution(mesh):
    in_specs = (
        P(None, ("group", "dev"), None),
        P(None, ("group", "dev"), None),
        P(None, ("group", "dev"), None),
        P("dev", None, "group"),
        P("dev", None, "group"),
        P("dev", "group", None),
    )
    out_specs = P(None, ("group", "dev"), None)
    return jax.shard_map(local, mesh=mesh, in_specs=in_specs, out_specs=out_specs, check_vma=False)
```

profile of v0, /device:TPU:2, one launch (start us, length us, event | category | flops | bytes accessed | tf_op | source)
XLA Modules:
  0.0 669.3 jit_solution(3592615987225470911)
XLA Ops:
  6.5 0.0 copy-start
  6.5 0.0 all-gather.5.cloned.1.call-start
  6.5 0.8 slice_bitcast_fusion.3
  7.4 0.1 copy.65
  7.5 0.1 eq.125
  7.6 0.2 reduce_window_sum.18
  7.8 0.1 eq.129
  7.9 0.1 copy.58
  7.9 0.1 eq.114
  8.0 0.2 reduce_window_sum.17
  8.2 0.1 eq.118
  8.3 0.1 copy.57
  8.4 0.1 copy.64
  8.5 1.2 fusion.42
  9.7 0.1 broadcast_compare_fusion.1
  9.7 0.1 convert_reduce_fusion
  9.9 0.3 convolution_convert_fusion.3
  10.1 0.3 copy.60
  10.4 12.6 %all_to_all.20 = bf16[16,2,4096]{2,1,0:T(2,128)(2,1)} all-to-all(bf16[16,2,4096]{2,1,0:T(2,128)(2,1)S(1)} %copy.60), channel_id=1, replica_groups=mesh['group'=16,'dev'=16] {'dev'}, dimensions={0} | all-to-all | bytes 524288 | tf_op jit(solution)/shard_map/all_to_all | solution.py:30
  23.0 0.0 all-gather.5.cloned.1.call-update
  23.1 0.0 all-gather.7.cloned.1.call-start
  23.1 0.3 convolution_convert_fusion.2
  23.4 0.3 copy.67
  23.7 11.2 %all_to_all.21 = bf16[16,2,4096]{2,1,0:T(2,128)(2,1)} all-to-all(bf16[16,2,4096]{2,1,0:T(2,128)(2,1)S(1)} %copy.67), channel_id=1, replica_groups=mesh['group'=16,'dev'=16] {'dev'}, dimensions={0} | all-to-all | bytes 524288 | tf_op jit(solution)/shard_map/all_to_all | solution.py:30
  34.9 0.0 all-gather.7.cloned.1.call-update
  34.9 0.0 reduce-scatter.3.cloned.1.call-start
  35.0 88.3 %all-gather.5.cloned.1.call-done = bf16[256,2,4096]{2,1,0:T(2,128)(2,1)} async-done(((bf16[16,2,4096]{2,1,0:T(2,128)(2,1)}), bf16[256,2,4096]{2,1,0:T(2,128)(2,1)}) %all-gather.5.cloned.1.call-update) | async-done | bytes 4194320 | tf_op jit(solution)/shard_map/all_gather | solution.py:31
  123.3 7.2 %reshape.161 = bf16[512,4096]{1,0:T(8,128)(2,1)} reshape(bf16[256,2,4096]{2,1,0:T(2,128)(2,1)} %all-gather.5.cloned.1.call-done) | data formatting | bytes 8388608 | tf_op jit(solution)/shard_map/reshape | solution.py:32
  130.5 0.0 copy-start.1
  130.5 0.0 copy-start.4
  130.5 5.6 fusion.12
  136.1 0.0 copy-done.1
  136.1 0.0 copy-done.4
  136.1 2.3 fusion.23
  138.5 0.9 dot_general.44
  139.4 0.0 copy-done
  139.4 5.3 convolution_convert_fusion.1
  144.7 0.0 reduce-scatter.3.cloned.1.call-update
  144.8 0.2 reduce-scatter.5.cloned.1.call-start
  145.0 77.3 %all-gather.7.cloned.1.call-done = bf16[256,2,4096]{2,1,0:T(2,128)(2,1)} async-done(((bf16[16,2,4096]{2,1,0:T(2,128)(2,1)}), bf16[256,2,4096]{2,1,0:T(2,128)(2,1)}) %all-gather.7.cloned.1.call-update) | async-done | bytes 4194320 | tf_op jit(solution)/shard_map/all_gather | solution.py:31
  222.3 7.2 %reshape.162 = bf16[512,4096]{1,0:T(8,128)(2,1)} reshape(bf16[256,2,4096]{2,1,0:T(2,128)(2,1)} %all-gather.7.cloned.1.call-done) | data formatting | bytes 8388608 | tf_op jit(solution)/shard_map/reshape | solution.py:32
  229.5 5.6 fusion.10
  235.1 0.0 copy-done.2
  235.1 0.0 copy-done.5
  235.1 2.3 fusion.20
  237.5 0.9 dot_general.51
  238.4 5.3 convolution_convert_fusion
  243.7 0.0 reduce-scatter.5.cloned.1.call-update
  243.7 189.8 %reduce-scatter.3.cloned.1.call-done = bf16[1,16,2,4096]{3,1,2,0:T(8,128)(2,1)} async-done(((bf16[16,16,2,4096]{3,1,2,0:T(8,128)(2,1)}), bf16[1,16,2,4096]{3,1,2,0:T(8,128)(2,1)}) %reduce-scatter.3.cloned.1.call-update) | async-done | bytes 262160 | tf_op jit(solution)/shard_map/reduce_scatter | solution.py:38
  433.5 1.9 copy.62
  435.5 5.9 all-to-all-start.1
  441.4 0.0 copy-done.3
  441.4 0.1 copy.73
  441.5 0.1 copy.77
  441.6 0.1 fusion.32
  441.7 204.5 %reduce-scatter.5.cloned.1.call-done = bf16[1,16,2,4096]{3,1,2,0:T(8,128)(2,1)} async-done(((bf16[16,16,2,4096]{3,1,2,0:T(8,128)(2,1)}), bf16[1,16,2,4096]{3,1,2,0:T(8,128)(2,1)}) %reduce-scatter.5.cloned.1.call-update) | async-done | bytes 262160 | tf_op jit(solution)/shard_map/reduce_scatter | solution.py:38
  646.2 1.9 copy.69
  648.1 0.0 all-to-all-done.1
  648.1 5.8 all-to-all-start.3
  653.8 0.1 fusion.30
  654.0 0.4 fusion.3
  654.4 6.4 all-to-all-done.3
  660.7 1.3 fusion.2
  662.1 0.7 copy.71
  (12 shorter events, 0.1 us)
Async XLA Ops:
  6.5 132.9 %copy-start = (bf16[1,384,4096]{2,1,0:T(8,128)(2,1)S(1)}, bf16[1,384,4096]{2,1,0:T(8,128)(2,1)}, u32[]{:S(2)}) copy-start(bf16[1,384,4096]{2,1,0:T(8,128)(2,1)} %param.11) | copy-start | bytes 9437188
  6.5 116.7 %all-gather.5.cloned.1.call-start = ((), (), s32[]{:S(2)}) async-start(), calls=%async_computation.8 | async-start | bytes 4456448 | tf_op jit(solution)/shard_map/all_gather | solution.py:31
  23.1 199.2 %all-gather.7.cloned.1.call-start = ((), (), s32[]{:S(2)}) async-start(), calls=%async_computation.9 | async-start | bytes 4456448 | tf_op jit(solution)/shard_map/all_gather | solution.py:31
  34.9 398.6 %reduce-scatter.3.cloned.1.call-start = ((), (), s32[]{:S(2)}) async-start(), calls=%async_computation.6 | async-start | bytes 4456448 | tf_op jit(solution)/shard_map/reduce_scatter | solution.py:38
  130.5 5.6 copy-start.1
  130.5 5.6 copy-start.4
  144.8 501.4 %reduce-scatter.5.cloned.1.call-start = ((), (), s32[]{:S(2)}) async-start(), calls=%async_computation.7 | async-start | bytes 4456448 | tf_op jit(solution)/shard_map/reduce_scatter | solution.py:38
  229.5 5.6 copy-start.2
  229.5 5.6 copy-start.5
  243.7 197.7 %copy-start.3 = (f32[2,6,2]{1,2,0:T(2,128)S(1)}, f32[2,6,2]{1,2,0:T(2,128)}, u32[]{:S(2)}) copy-start(f32[2,6,2]{1,2,0:T(2,128)} %param.8) | copy-start | bytes 292
  435.5 212.6 %all-to-all-start.1 = ((bf16[16,2,4096]{2,1,0:T(2,128)(2,1)}), bf16[16,2,4096]{2,1,0:T(2,128)(2,1)S(1)}, u32[]{:S(2)}, u32[]{:S(2)}) async-start(bf16[16,2,4096]{2,1,0:T(2,128)(2,1)} %copy.62), calls=%async_computation.2 | async-start | bytes 524288 | tf_op jit(solution)/shard_map/all_to_all | solution.py:42
  648.1 12.6 %all-to-all-start.3 = ((bf16[16,2,4096]{2,1,0:T(2,128)(2,1)}), bf16[16,2,4096]{2,1,0:T(2,128)(2,1)}, u32[]{:S(2)}, u32[]{:S(2)}) async-start(bf16[16,2,4096]{2,1,0:T(2,128)(2,1)} %copy.69), calls=%async_computation.5 | async-start | bytes 524288 | tf_op jit(solution)/shard_map/all_to_all | solution.py:42
Sparse Core Ops, SparseCore 0:
  23.2 100.0 all-gather.4
  125.9 96.3 all-gather.6
  226.3 207.1 reduce-scatter.2
  437.4 208.7 reduce-scatter.4
where the time goes:
time: 672 us; the launch traced here: 669 us
  waiting for transfers between devices  566 us (84%)
  matrix products  29 us (4%)
  local copies, waits for them, and re-layouts  24.3 us (4%)
  blocking collectives  23.8 us (4%)
  between operations  13.3 us (2%)
  starting transfers between devices  12 us (2%)
    reduce_scatter x2, waiting for transfers between devices, local(): lax.psum_scatter(partial_value.astype(jnp.bfloat16), 'group', scatter_dim...  394 us
    all_gather x2, waiting for transfers between devices, local(): shard_piece = lax.all_gather(incoming[None], 'group', axis=0, tiled=True)  166 us
    all_to_all x2, blocking collectives, local(): lax.all_to_all(outgoing, 'dev', split_axis=0, concat_axis=0, tiled=True)  23.8 us
    reshape x2, local copies, waits for them, and re-layouts, local(): flat_rows = shard_piece.reshape(-1, shard_piece.shape[-1])  14.4 us
  transfers between devices with their start and end apart: 6, of which 5 were waited for; matrix products, arithmetic and copies ran while one was open for 7% of the time, Pallas kernels for 0%

commit v1 on v0

v1 whole, which is shorter than its diff:
```python
import jax
import jax.numpy as jnp
from jax import lax
from jax.experimental import pallas as pl
from jax.experimental.pallas import tpu as pltpu
from jax.sharding import PartitionSpec as P

MESH = pl.DeviceIdType.MESH
NX, NY, NZ = 4, 4, 8
D, FFD = 4096, 384
BLK = 64
NC = 4
CW = D // NC
HDR = 128
POS = {0: 0, 1: 1, 7: 2, 2: 3, 6: 4, 3: 5, 5: 6, 4: 7}
GROUPS = ((0, 3), (3, 2), (5, 2), (7, 1))


def kernel(
    msg, wmat, perm, gate, up, down, out,
    raw, hdr_t, sel, xs, wg, wu, wd, h, p, sp, rp, fin, yb, pb, xb,
    own_sem, w_own, w_send, w_recv, x_send, x_recv, y_send, y_recv, y_own,
    g_send, g_recv, r_send, r_recv, b_send, b_recv, b_own, f_send, f_recv, f_own,
):
    g, d = lax.axis_index("group"), lax.axis_index("dev")
    z, x_hi = lax.rem(g, NZ), g // NZ
    core, y, x_lo = lax.rem(d, 2), lax.rem(d // 2, NY), d // (2 * NY)
    x = x_hi * 2 + x_lo

    def dev(xx, yy, zz, cc):
        return ((xx // 2) * NZ + zz, (lax.rem(xx, 2) * NY + yy) * 2 + cc)

    def x_at(j):
        return dev(lax.rem(x + j, NX), y, z, core)

    def y_at(j):
        return dev(x, lax.rem(y + j, NY), z, core)

    def z_at(j):
        return dev(x, y, lax.rem(z + j, NZ), core)

    other = dev(x, y, z, 1 - core)

    def remote(src, dst, send, recv, to):
        return pltpu.make_async_remote_copy(
            src_ref=src, dst_ref=dst, send_sem=send, recv_sem=recv, device_id=to, device_id_type=MESH
        )

    def cols(c):
        return pl.ds(c * CW, CW)

    def rows16(i):
        return pl.ds(pl.multiple_of(i * 16, 16), 16)

    sends = []

    def start(copy):
        copy.start()
        sends.append(copy)

    own = pltpu.make_async_copy(msg, raw.at[pl.ds(0, 16), :], own_sem)
    own.start()
    w_copies = [
        pltpu.make_async_copy(gate, wg.at[:, pl.ds(0, FFD)], w_own.at[0]),
        pltpu.make_async_copy(up, wu.at[:, pl.ds(0, FFD)], w_own.at[1]),
        pltpu.make_async_copy(down, wd.at[pl.ds(0, FFD), :], w_own.at[2]),
    ]
    barrier = pltpu.get_barrier_semaphore()
    partners = [x_at(j) for j in (1, 2, 3)] + [y_at(j) for j in (1, 2, 3)] + [z_at(1), z_at(NZ - 1), other]
    for partner in partners:
        pl.semaphore_signal(barrier, inc=1, device_id=partner, device_id_type=MESH)
    pl.semaphore_wait(barrier, len(partners))

    def x_copy(j, c):
        part = pl.ds(D, HDR) if c == NC else cols(c)
        return remote(
            msg.at[:, part], raw.at[pl.ds(j * 16, 16), part], x_send.at[j - 1, c], x_recv.at[j - 1, c], x_at(j)
        )

    x_copies = {}
    for c in (NC, 0, 1, 2, 3):
        for j in (1, 3, 2):
            x_copies[j, c] = x_copy(j, c)
            start(x_copies[j, c])
    for copy in w_copies:
        copy.start()
    w_remote = [
        remote(gate, wg.at[:, pl.ds(FFD, FFD)], w_send.at[0], w_recv.at[0], other),
        remote(up, wu.at[:, pl.ds(FFD, FFD)], w_send.at[1], w_recv.at[1], other),
        remote(down, wd.at[pl.ds(FFD, FFD), :], w_send.at[2], w_recv.at[2], other),
    ]
    for copy in w_remote:
        start(copy)

    y_copies = {}

    def pick(c):
        if c == 0:
            own.wait()
            for j in (1, 2, 3):
                x_copies[j, NC].wait_recv()
            hdr_t[...] = raw[:, pl.ds(D, HDR)].astype(jnp.float32).T.astype(jnp.bfloat16)
        for j in (1, 2, 3):
            x_copies[j, c].wait_recv()
        sel[:, cols(c)] = jnp.dot(
            hdr_t[...], raw[:, cols(c)], preferred_element_type=jnp.float32
        ).astype(jnp.bfloat16)
        for j in (1, 3, 2):
            to = lax.rem(y + j, NY)
            y_copies[j, c] = remote(
                sel.at[rows16(x_lo * 4 + to), cols(c)], xs.at[rows16(y), cols(c)],
                y_send.at[j - 1, c], y_recv.at[j - 1, c], y_at(j),
            )
            start(y_copies[j, c])
        y_copies[0, c] = pltpu.make_async_copy(
            sel.at[rows16(x_lo * 4 + y), cols(c)], xs.at[rows16(y), cols(c)], y_own.at[c]
        )
        y_copies[0, c].start()

    def block(k):
        return pl.ds(POS[k] * BLK, BLK)

    def g_copy(way, hop, c):
        k_from, k_to = ((NZ - hop) % NZ, NZ - hop - 1) if way == 0 else (hop, hop + 1)
        return remote(
            xs.at[block(k_from), cols(c)], xs.at[block(k_to), cols(c)],
            g_send.at[way, hop, c], g_recv.at[way, hop, c], z_at(1 if way == 0 else NZ - 1),
        )

    def far(way):
        return (0, 1) if way == 0 else (2, 3)

    g_copies = {}

    def g_start(way, hop, c):
        g_copies[way, hop, c] = g_copy(way, hop, c)
        start(g_copies[way, hop, c])

    order = {0: (0, 1, 2, 3), 1: (2, 3, 0, 1)}

    def z_first(c):
        for j in (1, 2, 3):
            y_copies[j, c].wait_recv()
        y_copies[0, c].wait()
        for way in (0, 1):
            g_start(way, 0, c)

    def z_next(hop, which):
        for i in which:
            for way in (0, 1):
                c = order[way][i]
                if hop == 3 and c not in far(way):
                    continue
                g_copies[way, hop, c].wait_recv()
                if hop < 2 or (hop == 2 and c in far(way)):
                    g_start(way, hop + 1, c)

    pick(0)
    pick(1)
    z_first(0)
    pick(2)
    z_first(1)
    pick(3)
    z_first(2)
    z_first(3)

    def gate_up(group):
        first, count = GROUPS[group]
        rows, live = pl.ds(first * BLK, count * BLK), pl.ds(0, count * BLK)

        def tile(n, carry):
            part = pl.ds(pl.multiple_of(n * 256, 256), 256)
            gate_val = jnp.dot(xs[rows, :], wg[:, part], preferred_element_type=jnp.float32)
            up_val = jnp.dot(xs[rows, :], wu[:, part], preferred_element_type=jnp.float32)
            h[live, part] = (jax.nn.silu(gate_val) * up_val).astype(jnp.bfloat16)
            return carry

        lax.fori_loop(0, 2 * FFD // 256, tile, 0)

    def down_proj(group):
        first, count = GROUPS[group]
        rows, live = pl.ds(first * BLK, count * BLK), pl.ds(0, count * BLK)

        def tile(n, carry):
            part = pl.ds(pl.multiple_of(n * 256, 256), 256)
            p[rows, part] = jnp.dot(h[live, :], wd[:, part], preferred_element_type=jnp.float32)
            return carry

        lax.fori_loop(0, D // 256, tile, 0)

    z_next(0, (0, 1, 2, 3))
    for copy in w_copies:
        copy.wait()
    for copy in w_remote:
        copy.wait_recv()
    gate_up(0)
    z_next(1, (0, 1))
    down_proj(0)
    z_next(1, (2, 3))
    gate_up(1)
    z_next(2, (0, 1))
    down_proj(1)
    z_next(2, (2, 3))
    gate_up(2)
    down_proj(2)

    def held(way, hop):
        return 4 - hop if way == 0 else (4 + hop) % NZ

    r_copies = {}

    def r_start(way, hop, c):
        r_copies[way, hop, c] = remote(
            sp.at[way, hop, :, cols(c)], rp.at[way, hop, :, cols(c)],
            r_send.at[way, hop, c], r_recv.at[way, hop, c], z_at(1 if way == 0 else NZ - 1),
        )
        start(r_copies[way, hop, c])

    def r_own(way, hop, c):
        sp[way, hop, :, cols(c)] = p[block(held(way, hop)), cols(c)].astype(jnp.bfloat16)
        r_start(way, hop, c)

    def r_add(way, hop, c):
        r_copies[way, hop - 1, c].wait_recv()
        sp[way, hop, :, cols(c)] = (
            p[block(held(way, hop)), cols(c)] + rp[way, hop - 1, :, cols(c)].astype(jnp.float32)
        ).astype(jnp.bfloat16)
        r_start(way, hop, c)

    near = {0: (2, 3), 1: (0, 1)}
    for i in (0, 1):
        for way in (0, 1):
            r_own(way, 1, near[way][i])
    z_next(3, (0, 1))
    gate_up(3)
    down_proj(3)
    for i in (0, 1):
        for way in (0, 1):
            r_own(way, 0, far(way)[i])
    for hop in (1, 2, 3):
        for which, step in ((near, hop + 1), ({0: far(0), 1: far(1)}, hop)):
            if step > 3:
                continue
            for i in (0, 1):
                for way in (0, 1):
                    r_add(way, step, which[way][i])

    b_copies = {}

    def back_y(c):
        for way in (0, 1):
            r_copies[way, 3, c].wait_recv()
        fin[:, cols(c)] = (
            p[block(0), cols(c)]
            + rp[0, 3, :, cols(c)].astype(jnp.float32)
            + rp[1, 3, :, cols(c)].astype(jnp.float32)
        ).astype(jnp.bfloat16)
        for j in (1, 3, 2):
            to = lax.rem(y + j, NY)
            b_copies[j, c] = remote(
                fin.at[rows16(to), cols(c)], yb.at[rows16(y), cols(c)],
                b_send.at[j - 1, c], b_recv.at[j - 1, c], y_at(j),
            )
            start(b_copies[j, c])
        b_copies[0, c] = pltpu.make_async_copy(
            fin.at[rows16(y), cols(c)], yb.at[rows16(y), cols(c)], b_own.at[c]
        )
        b_copies[0, c].start()

    f_copies = {}

    def back_x(c):
        for j in (1, 2, 3):
            b_copies[j, c].wait_recv()
        b_copies[0, c].wait()
        pb[:, cols(c)] = jnp.dot(perm[...], yb[:, cols(c)], preferred_element_type=jnp.float32).astype(jnp.bfloat16)
        for j in (1, 3, 2):
            to = lax.rem(x + j, NX)
            f_copies[j, c] = remote(
                pb.at[rows16(to), cols(c)], xb.at[rows16(x), cols(c)],
                f_send.at[j - 1, c], f_recv.at[j - 1, c], x_at(j),
            )
            start(f_copies[j, c])
        f_copies[0, c] = pltpu.make_async_copy(
            pb.at[rows16(x), cols(c)], xb.at[rows16(x), cols(c)], f_own.at[c]
        )
        f_copies[0, c].start()

    def finish(c):
        for j in (1, 2, 3):
            f_copies[j, c].wait_recv()
        f_copies[0, c].wait()
        out[:, cols(c)] = jnp.dot(
            wmat[...], xb[:, cols(c)].astype(jnp.float32),
            preferred_element_type=jnp.float32, precision=lax.Precision.HIGHEST,
        ).astype(jnp.bfloat16)

    back_y(0)
    back_y(2)
    back_x(0)
    back_y(1)
    back_x(2)
    back_y(3)
    finish(0)
    back_x(1)
    finish(2)
    back_x(3)
    finish(1)
    finish(3)
    for copy in sends:
        copy.wait_send()


def local(expert_input, expert_ids, combine, gate_weight, up_weight, down_weight):
    steps, rows = expert_input.shape[0], expert_input.shape[1]
    x = (lax.axis_index("group") // NZ) * 2 + lax.axis_index("dev") // (2 * NY)
    ids = expert_ids.reshape(steps, 2 * rows)
    order = jnp.arange(2 * rows)
    earlier = (ids[:, :, None] == ids[:, None, :]) & (order[None, :] < order[:, None])[None]
    slot = jnp.sum(earlier.astype(jnp.int32), 2) + 2 * jnp.arange(steps)[:, None]
    pad = ((0, 0), (0, 8 - rows), (0, 0))
    ids = jnp.pad(ids.reshape(steps, rows, 2), pad, constant_values=-1).reshape(16, 2)
    slot = jnp.pad(slot.reshape(steps, rows, 2), pad).reshape(16, 2)
    weight = jnp.pad(combine, pad).reshape(16, 2)
    place = (ids // 4) * 64 + lax.rem(ids, 4) * 16 + x * 4 + slot
    place = jnp.where(ids < 0, -1, place)
    header = jnp.any(place[:, :, None] == jnp.arange(HDR), 1).astype(jnp.bfloat16)
    col = jnp.arange(64)
    expert, col_slot = lax.rem(col // 16, 2) * 4 + lax.rem(col // 4, 4), lax.rem(col, 4)
    hit = (ids[:, :, None] == expert) & (slot[:, :, None] == col_slot)
    wmat = jnp.sum(jnp.where(hit, weight[:, :, None], 0.0), 1)
    perm = (
        ((col // 16)[:, None] == lax.rem(col // 4, 4)[None, :])
        & (lax.rem(col // 4, 4)[:, None] == (col // 16)[None, :])
        & (col_slot[:, None] == col_slot[None, :])
    ).astype(jnp.bfloat16)
    msg = jnp.concatenate([jnp.pad(expert_input, pad).reshape(16, D), header], 1)
    bf, vm = jnp.bfloat16, pltpu.VMEM
    dma = pltpu.SemaphoreType.DMA
    result = pl.pallas_call(
        kernel,
        out_shape=jax.ShapeDtypeStruct((16, D), bf),
        in_specs=[
            pl.BlockSpec(memory_space=pl.ANY),
            pl.BlockSpec(memory_space=pltpu.VMEM),
            pl.BlockSpec(memory_space=pltpu.VMEM),
            pl.BlockSpec(memory_space=pl.ANY),
            pl.BlockSpec(memory_space=pl.ANY),
            pl.BlockSpec(memory_space=pl.ANY),
        ],
        out_specs=pl.BlockSpec(memory_space=pltpu.VMEM),
        scratch_shapes=[
            vm((64, D + HDR), bf), vm((HDR, 64), bf), vm((HDR, D), bf), vm((NZ * BLK, D), bf),
            vm((D, 2 * FFD), bf), vm((D, 2 * FFD), bf), vm((2 * FFD, D), bf),
            vm((3 * BLK, 2 * FFD), bf), vm((NZ * BLK, D), jnp.float32),
            vm((2, 4, BLK, D), bf), vm((2, 4, BLK, D), bf),
            vm((BLK, D), bf), vm((64, D), bf), vm((64, D), bf), vm((64, D), bf),
            dma, dma((3,)), dma((3,)), dma((3,)),
            dma((3, NC + 1)), dma((3, NC + 1)), dma((3, NC)), dma((3, NC)), dma((NC,)),
            dma((2, 4, NC)), dma((2, 4, NC)), dma((2, 4, NC)), dma((2, 4, NC)),
            dma((3, NC)), dma((3, NC)), dma((NC,)), dma((3, NC)), dma((3, NC)), dma((NC,)),
        ],
        compiler_params=pltpu.CompilerParams(
            collective_id=0, has_side_effects=True, vmem_limit_bytes=60 * 2**20
        ),
    )(msg, wmat, perm, gate_weight[0], up_weight[0], down_weight[0])
    return result.reshape(steps, 8, D)[:, :rows]


def solution(mesh):
    in_specs = (
        P(None, ("group", "dev"), None),
        P(None, ("group", "dev"), None),
        P(None, ("group", "dev"), None),
        P("dev", None, "group"),
        P("dev", None, "group"),
        P("dev", "group", None),
    )
    out_specs = P(None, ("group", "dev"), None)
    return jax.shard_map(local, mesh=mesh, in_specs=in_specs, out_specs=out_specs, check_vma=False)
```

time: 672 us -> 123 us (0.18)
  waiting for transfers between devices: 566 us -> 0 us
  Pallas kernels: 0 us -> 115 us
  matrix products: 29 us -> 0 us
  blocking collectives: 23.8 us -> 0 us
  local copies, waits for them, and re-layouts: 24.3 us -> 5.4 us
  between operations: 13.3 us -> 0.03 us
  starting transfers between devices: 12 us -> 0 us
    reduce_scatter x2 -> x0, waiting for transfers between devices: 394 us -> none  [local(): lax.psum_scatter(partial_value.astype(jnp.bfloat16), 'group', scatter_dim...]
    all_gather x2 -> x0, waiting for transfers between devices: 166 us -> none  [local(): shard_piece = lax.all_gather(incoming[None], 'group', axis=0, tiled=True)]
    pallas_call x0 -> x1, Pallas kernels: none -> 115 us  [local(): pl.pallas_call(kernel, out_shape=jax.ShapeDtypeStruct((16, D), bf), in_sp...]
    dot_general x12 -> x0, matrix products: 29 us -> none  [the longest x2 11.2 us: local(): jnp.dot(flat_rows, gate_weight[0], preferred_element_type=jnp.float32)]
    all_to_all x2 -> x0, blocking collectives: 23.8 us -> none  [local(): lax.all_to_all(outgoing, 'dev', split_axis=0, concat_axis=0, tiled=True)]
    reshape x2 -> x4, local copies, waits for them, and re-layouts: 14.4 us -> 0.2 us  [the longest x2 0.09 us: local(): slot = jnp.pad(slot.reshape(steps, rows, 2), pad).reshape(16, 2)]
    all_to_all x2 -> x0, starting transfers between devices: 11.7 us -> none  [local(): lax.all_to_all(halves, 'dev', split_axis=0, concat_axis=0, tiled=True)]
  transfers between devices with their start and end apart: 6 -> 0, of which waited for: 5 -> 0; matrix products, arithmetic and copies ran while one was open for 7% -> 0% of each run, Pallas kernels for 0% -> 0%
where the time goes in v1:
time: 123 us
  Pallas kernels  115 us (93%)
  local copies, waits for them, and re-layouts  5.4 us (4%)
  other arithmetic  2.58 us (2%)
    pallas_call x1, Pallas kernels, local(): pl.pallas_call(kernel, out_shape=jax.ShapeDtypeStruct((16, D), bf), in_sp...  115 us
    unnamed x5, local copies, waits for them, and re-layouts  4.75 us

profile of v1, /device:TPU:2, one launch (start us, length us, event | category | flops | bytes accessed | tf_op | source)
XLA Modules:
  0.0 123.0 jit_solution(3635117078715656731)
XLA Ops:
  0.0 0.8 copy.29
  0.8 0.1 eq.44
  0.9 0.1 copy.30
  1.0 0.3 fusion.1
  1.3 0.1 copy.31
  1.4 0.1 reduce_sum.21
  1.5 0.1 broadcast_add_fusion
  1.6 0.1 copy.35
  1.7 0.7 copy.38
  2.4 0.1 reshape.181
  2.5 0.1 fusion
  2.5 1.0 copy.37
  3.5 0.7 pad_maximum_fusion.msg
  4.2 0.7 copy.39
  4.9 0.1 broadcast_in_dim.19
  5.0 0.7 select_reduce_fusion.wmat
  5.7 0.7 and_convert_fusion.perm
  6.4 115.0 %shard_map.64 = bf16[16,4096]{1,0:T(8,128)(2,1)} custom-call(bf16[16,4224]{1,0:T(8,128)(2,1)} %pad_maximum_fusion.msg, f32[16,64]{1,0:T(8,128)} %select_reduce_fusion.wmat, bf16[64,64]{1,0:T(8,128)(2,1)} %and_convert_fusion.perm, bf16[4096,384]{1,0:T(8,128)(2,1)} %bitcast.13, bf16[4096,384]{1,0:T(8,128)(2,1)} %bitcast.14, bf16[384,4096]{1,0:T(8,128)(2,1)} %bitcast.15), custom_call_target="tpu_custom_call" | custom-call | tf_op jit(solution)/shard_map/pallas_call | solution.py:340
  121.4 1.6 %copy.36 = bf16[2,6,4096]{2,0,1:T(2,128)(2,1)} copy(bf16[2,6,4096]{2,1,0:T(8,128)(2,1)} %bitcast.16) | data formatting | bytes 196608
  (10 shorter events, 0.1 us)

commit v2 on v1

--- a/solution.py
+++ b/solution.py
@@ -10,17 +10,24 @@
 D, FFD = 4096, 384
 BLK = 64
 NC = 4
-CW = D // NC
+CW = 512
+PW = NC * CW
+RW = D - PW
 HDR = 128
+XW = HDR + RW
+MW = XW + HDR
 POS = {0: 0, 1: 1, 7: 2, 2: 3, 6: 4, 3: 5, 5: 6, 4: 7}
 GROUPS = ((0, 3), (3, 2), (5, 2), (7, 1))
 
 
 def kernel(
-    msg, wmat, perm, gate, up, down, out,
+    msg, wmat, gate, up, down, out,
     raw, hdr_t, sel, xs, wg, wu, wd, h, p, sp, rp, fin, yb, pb, xb,
+    perm, xr, selr, finr, ybr, pbr, xbr, pr, spr, rpr,
     own_sem, w_own, w_send, w_recv, x_send, x_recv, y_send, y_recv, y_own,
     g_send, g_recv, r_send, r_recv, b_send, b_recv, b_own, f_send, f_recv, f_own,
+    rz_send, rz_recv, rx_send, rx_recv, ry_send, ry_recv, ry_own,
+    rb_send, rb_recv, rb_own, rf_send, rf_recv, rf_own, rr_send, rr_recv,
 ):
     g, d = lax.axis_index("group"), lax.axis_index("dev")
     z, x_hi = lax.rem(g, NZ), g // NZ
@@ -58,8 +65,10 @@
         copy.start()
         sends.append(copy)
 
-    own = pltpu.make_async_copy(msg, raw.at[pl.ds(0, 16), :], own_sem)
+    own = pltpu.make_async_copy(msg.at[:, pl.ds(0, PW + HDR)], raw.at[pl.ds(0, 16), :], own_sem.at[0])
     own.start()
+    own_r = pltpu.make_async_copy(msg.at[:, pl.ds(PW, MW)], xr.at[0, pl.ds(0, 16), :], own_sem.at[1])
+    own_r.start()
     w_copies = [
         pltpu.make_async_copy(gate, wg.at[:, pl.ds(0, FFD)], w_own.at[0]),
         pltpu.make_async_copy(up, wu.at[:, pl.ds(0, FFD)], w_own.at[1]),
@@ -71,8 +80,74 @@
         pl.semaphore_signal(barrier, inc=1, device_id=partner, device_id_type=MESH)
     pl.semaphore_wait(barrier, len(partners))
 
+    a, b = lax.broadcasted_iota(jnp.int32, (64, 64), 0), lax.broadcasted_iota(jnp.int32, (64, 64), 1)
+    moved = (b & 3) | ((b >> 4) << 2) | (((b >> 2) & 3) << 4)
+    perm[...] = jnp.where(a == moved, 1.0, 0.0).astype(jnp.bfloat16)
+
+    rz_copies = {}
+
+    def rz_start(way, hop):
+        k_from, k_to = ((NZ - hop) % NZ, NZ - hop - 1) if way == 0 else (hop, hop + 1)
+        part = pl.ds(0, MW) if hop < 3 else pl.ds(way * (MW // 2), MW // 2)
+        rows = pl.ds(0, 16)
+        source = msg.at[:, pl.ds(PW, MW)] if hop == 0 else xr.at[k_from, rows, part]
+        rz_copies[way, hop] = remote(
+            source, xr.at[k_to, rows, part], rz_send.at[way, hop], rz_recv.at[way, hop], z_at(1 if way == 0 else NZ - 1)
+        )
+        start(rz_copies[way, hop])
+
+    rx_copies, ry_copies = {}, {}
+
+    def rx_start(k):
+        for j in (1, 3, 2):
+            part = pl.ds(0, XW)
+            source = msg.at[:, pl.ds(PW, XW)] if k == 0 else xr.at[k, pl.ds(0, 16), part]
+            rx_copies[k, j] = remote(
+                source, xr.at[k, pl.ds(j * 16, 16), part], rx_send.at[k, j - 1], rx_recv.at[k, j - 1], x_at(j)
+            )
+            start(rx_copies[k, j])
+
+    def rz_next(hop):
+        if hop == 3:
+            for way in (0, 1):
+                rz_copies[way, 3].wait_recv()
+            rx_start(4)
+            return
+        for way in (0, 1):
+            rz_copies[way, hop].wait_recv()
+            rz_start(way, hop + 1)
+        for way in (0, 1):
+            rx_start(NZ - hop - 1 if way == 0 else hop + 1)
+
+    def r_pick(k):
+        if k == 0:
+            own_r.wait()
+        for j in (1, 2, 3):
+            rx_copies[k, j].wait_recv()
+        hdr_t[...] = xr[k, :, pl.ds(0, HDR)].astype(jnp.float32).T.astype(jnp.bfloat16)
+        selr[k] = jnp.dot(
+            hdr_t[pl.ds(pl.multiple_of(x_lo * 64, 64), 64), :], xr[k, :, pl.ds(HDR, RW)],
+            preferred_element_type=jnp.float32,
+        ).astype(jnp.bfloat16)
+        target = xs.at[pl.ds(pl.multiple_of(POS[k] * BLK + y * 16, 16), 16), pl.ds(PW, RW)]
+        for j in (1, 3, 2):
+            ry_copies[k, j] = remote(
+                selr.at[k, rows16(lax.rem(y + j, NY)), :], target, ry_send.at[k, j - 1], ry_recv.at[k, j - 1], y_at(j)
+            )
+            start(ry_copies[k, j])
+        ry_copies[k, 0] = pltpu.make_async_copy(selr.at[k, rows16(y), :], target, ry_own.at[k])
+        ry_copies[k, 0].start()
+
+    def r_ready(k):
+        for j in (1, 2, 3):
+            ry_copies[k, j].wait_recv()
+        ry_copies[k, 0].wait()
+
+    for way in (0, 1):
+        rz_start(way, 0)
+
     def x_copy(j, c):
-        part = pl.ds(D, HDR) if c == NC else cols(c)
+        part = pl.ds(PW, HDR) if c == NC else cols(c)
         return remote(
             msg.at[:, part], raw.at[pl.ds(j * 16, 16), part], x_send.at[j - 1, c], x_recv.at[j - 1, c], x_at(j)
         )
@@ -82,6 +157,7 @@
         for j in (1, 3, 2):
             x_copies[j, c] = x_copy(j, c)
             start(x_copies[j, c])
+    rx_start(0)
     for copy in w_copies:
         copy.start()
     w_remote = [
@@ -99,21 +175,21 @@
             own.wait()
             for j in (1, 2, 3):
                 x_copies[j, NC].wait_recv()
-            hdr_t[...] = raw[:, pl.ds(D, HDR)].astype(jnp.float32).T.astype(jnp.bfloat16)
         for j in (1, 2, 3):
             x_copies[j, c].wait_recv()
+        hdr_t[...] = raw[:, pl.ds(PW, HDR)].astype(jnp.float32).T.astype(jnp.bfloat16)
         sel[:, cols(c)] = jnp.dot(
-            hdr_t[...], raw[:, cols(c)], preferred_element_type=jnp.float32
+            hdr_t[pl.ds(pl.multiple_of(x_lo * 64, 64), 64), :], raw[:, cols(c)], preferred_element_type=jnp.float32
         ).astype(jnp.bfloat16)
         for j in (1, 3, 2):
             to = lax.rem(y + j, NY)
             y_copies[j, c] = remote(
-                sel.at[rows16(x_lo * 4 + to), cols(c)], xs.at[rows16(y), cols(c)],
+                sel.at[rows16(to), cols(c)], xs.at[rows16(y), cols(c)],
                 y_send.at[j - 1, c], y_recv.at[j - 1, c], y_at(j),
             )
             start(y_copies[j, c])
         y_copies[0, c] = pltpu.make_async_copy(
-            sel.at[rows16(x_lo * 4 + y), cols(c)], xs.at[rows16(y), cols(c)], y_own.at[c]
+            sel.at[rows16(y), cols(c)], xs.at[rows16(y), cols(c)], y_own.at[c]
         )
         y_copies[0, c].start()
 
@@ -156,53 +232,35 @@
                     g_start(way, hop + 1, c)
 
     pick(0)
+    rz_next(0)
     pick(1)
     z_first(0)
+    rz_next(1)
     pick(2)
     z_first(1)
     pick(3)
+    rz_next(2)
     z_first(2)
     z_first(3)
-
-    def gate_up(group):
+    rz_next(3)
+
+    def gate_up(group, n):
         first, count = GROUPS[group]
-        rows, live = pl.ds(first * BLK, count * BLK), pl.ds(0, count * BLK)
+        rows, part = pl.ds(first * BLK, count * BLK), pl.ds(n * 256, 256)
+        gate_val = jnp.dot(xs[rows, :], wg[:, part], preferred_element_type=jnp.float32)
+        up_val = jnp.dot(xs[rows, :], wu[:, part], preferred_element_type=jnp.float32)
+        h[rows, part] = (jax.nn.silu(gate_val) * up_val).astype(jnp.bfloat16)
+
+    def down_proj(group, quarter):
+        first, count = GROUPS[group]
+        rows = pl.ds(first * BLK, count * BLK)
 
         def tile(n, carry):
             part = pl.ds(pl.multiple_of(n * 256, 256), 256)
-            gate_val = jnp.dot(xs[rows, :], wg[:, part], preferred_element_type=jnp.float32)
-            up_val = jnp.dot(xs[rows, :], wu[:, part], preferred_element_type=jnp.float32)
-            h[live, part] = (jax.nn.silu(gate_val) * up_val).astype(jnp.bfloat16)
+            p[rows, part] = jnp.dot(h[rows, :], wd[:, part], preferred_element_type=jnp.float32)
             return carry
 
-        lax.fori_loop(0, 2 * FFD // 256, tile, 0)
-
-    def down_proj(group):
-        first, count = GROUPS[group]
-        rows, live = pl.ds(first * BLK, count * BLK), pl.ds(0, count * BLK)
-
-        def tile(n, carry):
-            part = pl.ds(pl.multiple_of(n * 256, 256), 256)
-            p[rows, part] = jnp.dot(h[live, :], wd[:, part], preferred_element_type=jnp.float32)
-            return carry
-
-        lax.fori_loop(0, D // 256, tile, 0)
-
-    z_next(0, (0, 1, 2, 3))
-    for copy in w_copies:
-        copy.wait()
-    for copy in w_remote:
-        copy.wait_recv()
-    gate_up(0)
-    z_next(1, (0, 1))
-    down_proj(0)
-    z_next(1, (2, 3))
-    gate_up(1)
-    z_next(2, (0, 1))
-    down_proj(1)
-    z_next(2, (2, 3))
-    gate_up(2)
-    down_proj(2)
+        lax.fori_loop(quarter * 4, quarter * 4 + 4, tile, 0)
 
     def held(way, hop):
         return 4 - hop if way == 0 else (4 + hop) % NZ
@@ -228,23 +286,172 @@
         r_start(way, hop, c)
 
     near = {0: (2, 3), 1: (0, 1)}
+
+    def r_adds(which, step):
+        for i in (0, 1):
+            for way in (0, 1):
+                r_add(way, step, which[way][i])
+
+    rb_copies, rf_copies, rr_copies = {}, {}, {}
+
+    def r_back_y(k):
+        finr[k] = p[block(k), pl.ds(PW, RW)].astype(jnp.bfloat16)
+        for j in (1, 3, 2):
+            rb_copies[k, j] = remote(
+                finr.at[k, rows16(lax.rem(y + j, NY)), :], ybr.at[k, rows16(y), :],
+                rb_send.at[k, j - 1], rb_recv.at[k, j - 1], y_at(j),
+            )
+            start(rb_copies[k, j])
+        rb_copies[k, 0] = pltpu.make_async_copy(finr.at[k, rows16(y), :], ybr.at[k, rows16(y), :], rb_own.at[k])
+        rb_copies[k, 0].start()
+
+    def r_back_x(k):
+        for j in (1, 2, 3):
+            rb_copies[k, j].wait_recv()
+        rb_copies[k, 0].wait()
+        pbr[k] = jnp.dot(perm[...], ybr[k], preferred_element_type=jnp.float32).astype(jnp.bfloat16)
+        for j in (1, 3, 2):
+            rf_copies[k, j] = remote(
+                pbr.at[k, rows16(lax.rem(x + j, NX)), :], xbr.at[k, rows16(x), :],
+                rf_send.at[k, j - 1], rf_recv.at[k, j - 1], x_at(j),
+            )
+            start(rf_copies[k, j])
+        rf_copies[k, 0] = pltpu.make_async_copy(pbr.at[k, rows16(x), :], xbr.at[k, rows16(x), :], rf_own.at[k])
+        rf_copies[k, 0].start()
+
+    def r_weigh(k):
+        for j in (1, 2, 3):
+            rf_copies[k, j].wait_recv()
+        rf_copies[k, 0].wait()
+        weights = xr[k, pl.ds(0, 16), pl.ds(XW, HDR)]
+        values = xbr[k]
+        pr[k] = jnp.dot(weights, jnp.concatenate([values, values], 0), preferred_element_type=jnp.float32)
+
+    def rr_step(way, hop):
+        part = pl.ds(0, RW) if hop else pl.ds(way * (RW // 2), RW // 2)
+        k = held(way, hop)
+        total = pr[k, :, part]
+        if hop:
+            rr_copies[way, hop - 1].wait_recv()
+            if hop == 1:
+                half = pl.ds(way * (RW // 2), RW // 2)
+                pr[k, :, half] = pr[k, :, half] + rpr[way, 0, :, half].astype(jnp.float32)
+                total = pr[k, :, part]
+            else:
+                total = total + rpr[way, hop - 1, :, part].astype(jnp.float32)
+        spr[way, hop, :, part] = total.astype(jnp.bfloat16)
+        rr_copies[way, hop] = remote(
+            spr.at[way, hop, :, part], rpr.at[way, hop, :, part],
+            rr_send.at[way, hop], rr_recv.at[way, hop], z_at(1 if way == 0 else NZ - 1),
+        )
+        start(rr_copies[way, hop])
+
+    def rr_steps(hop):
+        for way in (0, 1):
+            rr_step(way, hop)
+
+    def r_finish():
+        for way in (0, 1):
+            rr_copies[way, 3].wait_recv()
+        out[:, pl.ds(PW, RW)] = (
+            pr[0] + rpr[0, 3].astype(jnp.float32) + rpr[1, 3].astype(jnp.float32)
+        ).astype(jnp.bfloat16)
+
+    r_pick(0)
+    z_next(0, (0,))
+    r_pick(7)
+    z_next(0, (1, 2))
+    r_pick(1)
+    z_next(0, (3,))
+    for copy in w_copies[:2]:
+        copy.wait()
+    for copy in w_remote[:2]:
+        copy.wait_recv()
+    for k in (0, 7, 1):
+        r_ready(k)
+    gate_up(0, 0)
+    r_pick(6)
+    z_next(1, (0,))
+    gate_up(0, 1)
+    z_next(1, (1,))
+    r_pick(2)
+    gate_up(0, 2)
+    w_copies[2].wait()
+    w_remote[2].wait_recv()
+    z_next(1, (2,))
+    down_proj(0, 0)
+    down_proj(0, 1)
+    z_next(1, (3,))
+    r_pick(5)
+    down_proj(0, 2)
+    down_proj(0, 3)
+    r_ready(6)
+    r_ready(2)
+    gate_up(1, 0)
+    z_next(2, (0,))
+    r_pick(3)
+    gate_up(1, 1)
+    z_next(2, (1,))
+    r_pick(4)
+    gate_up(1, 2)
+    z_next(2, (2,))
+    for k in (0, 7, 1):
+        r_back_y(k)
+    down_proj(1, 0)
+    down_proj(1, 1)
+    z_next(2, (3,))
+    down_proj(1, 2)
+    down_proj(1, 3)
+    r_ready(5)
+    r_ready(3)
+    r_back_y(6)
+    r_back_y(2)
+    gate_up(2, 0)
+    r_back_x(0)
+    gate_up(2, 1)
+    r_back_x(7)
+    gate_up(2, 2)
+    r_back_x(1)
+    for quarter in range(4):
+        down_proj(2, quarter)
     for i in (0, 1):
         for way in (0, 1):
             r_own(way, 1, near[way][i])
+    r_back_y(5)
+    r_back_y(3)
     z_next(3, (0, 1))
-    gate_up(3)
-    down_proj(3)
-    for i in (0, 1):
-        for way in (0, 1):
-            r_own(way, 0, far(way)[i])
-    for hop in (1, 2, 3):
-        for which, step in ((near, hop + 1), ({0: far(0), 1: far(1)}, hop)):
-            if step > 3:
-                continue
-            for i in (0, 1):
-                for way in (0, 1):
-                    r_add(way, step, which[way][i])
-
+    r_ready(4)
+    gate_up(3, 0)
+    r_back_x(6)
+    gate_up(3, 1)
+    r_back_x(2)
+    gate_up(3, 2)
+    down_proj(3, 0)
+    r_own(0, 0, 0)
+    down_proj(3, 1)
+    r_own(0, 0, 1)
+    down_proj(3, 2)
+    r_own(1, 0, 2)
+    down_proj(3, 3)
+    r_own(1, 0, 3)
+    r_back_y(4)
+    r_back_x(5)
+    r_back_x(3)
+    r_adds(near, 2)
+    for k in (0, 7, 1):
+        r_weigh(k)
+    r_adds({0: far(0), 1: far(1)}, 1)
+    r_back_x(4)
+    for k in (6, 2):
+        r_weigh(k)
+    r_adds(near, 3)
+    for k in (5, 3):
+        r_weigh(k)
+    r_adds({0: far(0), 1: far(1)}, 2)
+    r_weigh(4)
+    rr_steps(0)
+    r_adds({0: far(0), 1: far(1)}, 3)
+    rr_steps(1)
     b_copies = {}
 
     def back_y(c):
@@ -297,14 +504,17 @@
 
     back_y(0)
     back_y(2)
+    rr_steps(2)
     back_x(0)
     back_y(1)
     back_x(2)
     back_y(3)
+    rr_steps(3)
     finish(0)
     back_x(1)
     finish(2)
     back_x(3)
+    r_finish()
     finish(1)
     finish(3)
     for copy in sends:
@@ -329,12 +539,11 @@
     expert, col_slot = lax.rem(col // 16, 2) * 4 + lax.rem(col // 4, 4), lax.rem(col, 4)
     hit = (ids[:, :, None] == expert) & (slot[:, :, None] == col_slot)
     wmat = jnp.sum(jnp.where(hit, weight[:, :, None], 0.0), 1)
-    perm = (
-        ((col // 16)[:, None] == lax.rem(col // 4, 4)[None, :])
-        & (lax.rem(col // 4, 4)[:, None] == (col // 16)[None, :])
-        & (col_slot[:, None] == col_slot[None, :])
-    ).astype(jnp.bfloat16)
-    msg = jnp.concatenate([jnp.pad(expert_input, pad).reshape(16, D), header], 1)
+    high = lax.reduce_precision(wmat, 8, 7)
+    rows_in = jnp.pad(expert_input, pad).reshape(16, D)
+    msg = jnp.concatenate(
+        [rows_in[:, :PW], header, rows_in[:, PW:], high.astype(jnp.bfloat16), (wmat - high).astype(jnp.bfloat16)], 1
+    )
     bf, vm = jnp.bfloat16, pltpu.VMEM
     dma = pltpu.SemaphoreType.DMA
     result = pl.pallas_call(
@@ -343,27 +552,31 @@
         in_specs=[
             pl.BlockSpec(memory_space=pl.ANY),
             pl.BlockSpec(memory_space=pltpu.VMEM),
-            pl.BlockSpec(memory_space=pltpu.VMEM),
             pl.BlockSpec(memory_space=pl.ANY),
             pl.BlockSpec(memory_space=pl.ANY),
             pl.BlockSpec(memory_space=pl.ANY),
         ],
         out_specs=pl.BlockSpec(memory_space=pltpu.VMEM),
         scratch_shapes=[
-            vm((64, D + HDR), bf), vm((HDR, 64), bf), vm((HDR, D), bf), vm((NZ * BLK, D), bf),
+            vm((64, PW + HDR), bf), vm((HDR, 64), bf), vm((64, PW), bf), vm((NZ * BLK, D), bf),
             vm((D, 2 * FFD), bf), vm((D, 2 * FFD), bf), vm((2 * FFD, D), bf),
-            vm((3 * BLK, 2 * FFD), bf), vm((NZ * BLK, D), jnp.float32),
-            vm((2, 4, BLK, D), bf), vm((2, 4, BLK, D), bf),
-            vm((BLK, D), bf), vm((64, D), bf), vm((64, D), bf), vm((64, D), bf),
-            dma, dma((3,)), dma((3,)), dma((3,)),
+            vm((NZ * BLK, 2 * FFD), bf), vm((NZ * BLK, D), jnp.float32),
+            vm((2, 4, BLK, PW), bf), vm((2, 4, BLK, PW), bf),
+            vm((BLK, PW), bf), vm((64, PW), bf), vm((64, PW), bf), vm((64, PW), bf),
+            vm((64, 64), bf), vm((NZ, 64, MW), bf),
+            vm((NZ, 64, RW), bf), vm((NZ, 64, RW), bf), vm((NZ, 64, RW), bf), vm((NZ, 64, RW), bf), vm((NZ, 64, RW), bf),
+            vm((NZ, 16, RW), jnp.float32), vm((2, 4, 16, RW), bf), vm((2, 4, 16, RW), bf),
+            dma((2,)), dma((3,)), dma((3,)), dma((3,)),
             dma((3, NC + 1)), dma((3, NC + 1)), dma((3, NC)), dma((3, NC)), dma((NC,)),
             dma((2, 4, NC)), dma((2, 4, NC)), dma((2, 4, NC)), dma((2, 4, NC)),
             dma((3, NC)), dma((3, NC)), dma((NC,)), dma((3, NC)), dma((3, NC)), dma((NC,)),
+            dma((2, 4)), dma((2, 4)), dma((NZ, 3)), dma((NZ, 3)), dma((NZ, 3)), dma((NZ, 3)), dma((NZ,)),
+            dma((NZ, 3)), dma((NZ, 3)), dma((NZ,)), dma((NZ, 3)), dma((NZ, 3)), dma((NZ,)), dma((2, 4)), dma((2, 4)),
         ],
         compiler_params=pltpu.CompilerParams(
-            collective_id=0, has_side_effects=True, vmem_limit_bytes=60 * 2**20
+            collective_id=0, has_side_effects=True, vmem_limit_bytes=63 * 2**20
         ),
-    )(msg, wmat, perm, gate_weight[0], up_weight[0], down_weight[0])
+    )(msg, wmat, gate_weight[0], up_weight[0], down_weight[0])
     return result.reshape(steps, 8, D)[:, :rows]
 
 

time: 123 us -> 114 us (0.927)
  Pallas kernels: 115 us -> 107 us
  other arithmetic: 2.58 us -> 0.63 us
    pallas_call x1, Pallas kernels: 115 us -> 107 us  [local(): pl.pallas_call(kernel, out_shape=jax.ShapeDtypeStruct((16, D), bf), in_sp...]
    unnamed x5 -> x7, local copies, waits for them, and re-layouts: 4.75 us -> 4.75 us
where the time goes in v2:
time: 114 us; the launch traced here: 113 us
  Pallas kernels  107 us (94%)
  local copies, waits for them, and re-layouts  6.14 us (5%)
    pallas_call x1, Pallas kernels, local(): pl.pallas_call(kernel, out_shape=jax.ShapeDtypeStruct((16, D), bf), in_sp...  107 us
    unnamed x7, local copies, waits for them, and re-layouts  4.75 us

profile of v2, /device:TPU:2, one launch (start us, length us, event | category | flops | bytes accessed | tf_op | source)
XLA Modules:
  0.0 113.4 jit_solution(9343314406877786616)
XLA Ops:
  0.0 0.7 copy.39
  0.7 0.1 broadcast_in_dim.27
  0.8 0.7 copy.38
  1.5 0.1 reshape.117
  1.6 0.8 copy.29
  2.3 0.1 eq.26
  2.4 0.1 copy.30
  2.5 0.3 fusion.1
  2.9 0.1 copy.31
  3.0 0.1 reduce_sum.21
  3.0 0.1 broadcast_add_fusion
  3.1 0.1 copy.35
  3.2 0.1 fusion
  3.3 0.1 select_reduce_fusion.wmat
  3.4 0.0 copy-start
  3.4 1.0 copy.37
  4.5 0.7 concatenate.3.msg
  5.2 0.0 copy-done
  5.2 106.5 %shard_map.64 = bf16[16,4096]{1,0:T(8,128)(2,1)} custom-call(bf16[16,4352]{1,0:T(8,128)(2,1)} %concatenate.3.msg, f32[16,64]{1,0:T(8,128)} %copy-done, bf16[4096,384]{1,0:T(8,128)(2,1)} %bitcast.13, bf16[4096,384]{1,0:T(8,128)(2,1)} %bitcast.14, bf16[384,4096]{1,0:T(8,128)(2,1)} %bitcast.15), custom_call_target="tpu_custom_call" | custom-call | tf_op jit(solution)/shard_map/pallas_call | solution.py:549
  111.7 1.6 %copy.36 = bf16[2,6,4096]{2,0,1:T(2,128)(2,1)} copy(bf16[2,6,4096]{2,1,0:T(8,128)(2,1)} %bitcast.16) | data formatting | bytes 196608
  (11 shorter events, 0.1 us)
Async XLA Ops:
  3.4 1.8 %copy-start = (f32[16,64]{1,0:T(8,128)}, f32[16,64]{1,0:T(8,128)S(1)}, u32[]{:S(2)}) copy-start(f32[16,64]{1,0:T(8,128)S(1)} %select_reduce_fusion.wmat) | copy-start | bytes 12292

commit v3 on v2

--- a/solution.py
+++ b/solution.py
@@ -10,7 +10,7 @@
 D, FFD = 4096, 384
 BLK = 64
 NC = 4
-CW = 512
+CW = 640
 PW = NC * CW
 RW = D - PW
 HDR = 128

time: 114 us -> 111 us (0.974)
  Pallas kernels: 107 us -> 104 us
    pallas_call x1, Pallas kernels: 107 us -> 104 us  [local(): pl.pallas_call(kernel, out_shape=jax.ShapeDtypeStruct((16, D), bf), in_sp...]
where the time goes in v3:
time: 111 us; the launch traced here: 110 us
  Pallas kernels  104 us (94%)
  local copies, waits for them, and re-layouts  6.14 us (6%)
    pallas_call x1, Pallas kernels, local(): pl.pallas_call(kernel, out_shape=jax.ShapeDtypeStruct((16, D), bf), in_sp...  104 us
    unnamed x7, local copies, waits for them, and re-layouts  4.75 us

profile of v3, /device:TPU:2, one launch (start us, length us, event | category | flops | bytes accessed | tf_op | source)
XLA Modules:
  0.0 110.4 jit_solution(13047836826869119739)
XLA Ops:
  0.0 0.7 copy.39
  0.7 0.1 broadcast_in_dim.27
  0.8 0.7 copy.38
  1.5 0.1 reshape.117
  1.6 0.8 copy.29
  2.3 0.1 eq.26
  2.4 0.1 copy.30
  2.5 0.3 fusion.1
  2.9 0.1 copy.31
  3.0 0.1 reduce_sum.21
  3.0 0.1 broadcast_add_fusion
  3.1 0.1 copy.35
  3.2 0.1 fusion
  3.3 0.1 select_reduce_fusion.wmat
  3.4 0.0 copy-start
  3.4 1.0 copy.37
  4.5 0.7 concatenate.3.msg
  5.2 0.0 copy-done
  5.2 103.6 %shard_map.64 = bf16[16,4096]{1,0:T(8,128)(2,1)} custom-call(bf16[16,4352]{1,0:T(8,128)(2,1)} %concatenate.3.msg, f32[16,64]{1,0:T(8,128)} %copy-done, bf16[4096,384]{1,0:T(8,128)(2,1)} %bitcast.13, bf16[4096,384]{1,0:T(8,128)(2,1)} %bitcast.14, bf16[384,4096]{1,0:T(8,128)(2,1)} %bitcast.15), custom_call_target="tpu_custom_call" | custom-call | tf_op jit(solution)/shard_map/pallas_call | solution.py:549
  108.8 1.6 %copy.36 = bf16[2,6,4096]{2,0,1:T(2,128)(2,1)} copy(bf16[2,6,4096]{2,1,0:T(8,128)(2,1)} %bitcast.16) | data formatting | bytes 196608
  (12 shorter events, 0.1 us)
Async XLA Ops:
  3.4 1.8 %copy-start = (f32[16,64]{1,0:T(8,128)}, f32[16,64]{1,0:T(8,128)S(1)}, u32[]{:S(2)}) copy-start(f32[16,64]{1,0:T(8,128)S(1)} %select_reduce_fusion.wmat) | copy-start | bytes 12292
